TPU v7x, 512 devices: a whole 4x8x8 slice. The times are simulated.
512 devices in a mesh: items: 32 (over x, y), cents: 16 (over z, core).
Axes of the slice: x: 4, y: 8, z: 8, core: 2. Of those that a mesh axis runs over, the one named last changes fastest.
Arguments:
- embeddings: bfloat16 [61440, 1024], P('items')
- counts: int32 [32], P('items'), may hold values from 1152 to 1920, as said below
- centroids: bfloat16 [2048, 1024], P('cents')
Outputs:
- final_centroids: bfloat16 [2048, 1024], P('cents')
Inputs may be any that keep to these rules, and one draw needn't show every extreme that they name: The counts of replicas 0 to i-1 sum to 1536 * i plus an offset of at most 192 in either direction, reached both ways in every draw; all counts sum to 49152. Rows of a buffer past its count carry no data.
All inputs are finite; a program needn't handle non-finite values.
Results may differ from a plain program's by a relative error of at most 0.0112.
Values may be sent and summed in bfloat16 or wider, within the bound.
No kernel may reach another device: no remote copies, remote signals or barrier semaphores. Data moves between devices by JAX's collectives and lax.ppermute only.
A program may use at most 64 MiB of HBM per device.

v0:
```python
import jax
import jax.numpy as jnp
from jax import lax
from jax.sharding import PartitionSpec as P

D = 1024
ROWS_DEV = 1536
ITERS = 2
SPILL = 192
prior_count = 2.0


def prefix(part, axis, combine, identity):
    place = lax.axis_index(axis)
    gathered = lax.all_gather(part, axis)
    state = jnp.zeros_like(part) + jnp.asarray(identity, part.dtype)

    def one(hop, state):
        return combine(state, lax.dynamic_index_in_dim(gathered, hop, 0, False))

    return lax.fori_loop(0, place, one, state)


def with_halo(block, sides, width):
    for axis, dim in sides:
        count = lax.axis_size(axis)
        forward = [(i, i + 1) for i in range(count - 1)]
        backward = [(target, source) for source, target in forward]
        low = lax.ppermute(
            lax.slice_in_dim(block, block.shape[dim] - width, None, axis=dim), axis, forward
        )
        high = lax.ppermute(lax.slice_in_dim(block, 0, width, axis=dim), axis, backward)
        block = jnp.concatenate([low, block, high], axis=dim)
    return block


def add_counts(earlier, later):
    return earlier + later


def settle_rows(embeddings, counts):
    capacity = embeddings.shape[0]
    own_count = counts[0]
    position = lax.axis_index("items")
    before = prefix(counts, "items", add_counts, jnp.zeros((1,), jnp.int32))[0]
    excess_below = before - position * ROWS_DEV
    excess_here = excess_below + own_count - ROWS_DEV
    from_below = jnp.maximum(excess_below, 0)
    sent_down = jnp.maximum(-excess_below, 0)
    from_above = jnp.maximum(-excess_here, 0)
    tail_rows = lax.dynamic_slice_in_dim(embeddings, own_count - SPILL, SPILL, 0)
    edge_rows = jnp.concatenate([embeddings[:SPILL], tail_rows], axis=0)
    extended = with_halo(edge_rows, (("items", 0),), SPILL)
    lower_rows = extended[:SPILL]
    upper_rows = extended[3 * SPILL :]
    joined = jnp.concatenate([lower_rows, embeddings, upper_rows], axis=0)
    slot_ids = jnp.arange(ROWS_DEV, dtype=jnp.int32)
    kept_rows = ROWS_DEV - from_below - from_above
    source = jnp.where(
        slot_ids < from_below,
        SPILL - from_below + slot_ids,
        jnp.where(
            slot_ids < from_below + kept_rows,
            SPILL + sent_down + slot_ids - from_below,
            SPILL + capacity + slot_ids - from_below - kept_rows,
        ),
    )
    return jnp.take(joined, source, axis=0)


def body(embeddings, counts, centroids):
    settled = settle_rows(embeddings, counts)
    scale = D ** (-0.5)
    current = centroids
    for step in range(ITERS):
        cent_f = current.astype(jnp.float32)
        norms = jnp.sum(cent_f * cent_f, axis=1)
        dots = lax.dot_general(
            settled, current, (((1,), (1,)), ((), ())), preferred_element_type=jnp.float32
        )
        score = (2.0 * dots - norms[None, :]) * scale
        top = lax.pmax(jnp.max(score, axis=1), "cents")
        expo = jnp.exp(score - top[:, None])
        total = lax.psum(jnp.sum(expo, axis=1), "cents")
        resp = (expo / total[:, None]).astype(jnp.bfloat16)
        mass_here = jnp.sum(resp.astype(jnp.float32), axis=0)
        moment_here = lax.dot_general(
            resp, settled, (((0,), (0,)), ((), ())), preferred_element_type=jnp.float32
        )
        moment, mass = lax.psum((moment_here, mass_here), "items")
        current = ((moment + prior_count * cent_f) / (mass[:, None] + prior_count)).astype(
            jnp.bfloat16
        )
    return current


def solution(mesh):
    in_specs = (P("items", None), P("items"), P("cents", None))
    out_specs = P("cents", None)
    return jax.shard_map(body, mesh=mesh, in_specs=in_specs, out_specs=out_specs, check_vma=False)
```

profile of v0, /device:TPU:64, one launch (start us, length us, event | category | flops | bytes accessed | tf_op | source)
XLA Modules:
  0.0 527.3 jit_solution(12058598038848635442)
XLA Ops:
  6.5 0.0 all-reduce.4.cloned.1.call-start
  7.2 1.3 constant_dynamic-slice_fusion.1
  8.5 3.5 collective-permute-start
  12.0 1.3 collective-permute-start.1
  13.3 1.3 dynamic-slice
  14.6 0.7 dynamic-update-slice
  15.4 25.5 %all-reduce = s32[32]{0:T(128)S(1)} all-reduce(s32[32]{0:T(128)S(1)} %dynamic-update-slice), channel_id=2, replica_groups=mesh['items'=32,'cents'=16] {'items'}, use_global_device_ids=true, to_apply=%add | all-reduce | flops 32 | bytes 256
  40.9 1.1 fusion.6
  42.0 0.0 collective-permute-done
  42.0 0.0 collective-permute-done.1
  42.0 3.9 pad_maximum_fusion
  46.0 0.0 copy-start
  46.0 10.8 %gather_fusion = bf16[1536,1024]{1,0:T(8,128)(2,1)} fusion(bf16[2304,1024]{1,0:T(8,128)(2,1)} %pad_maximum_fusion, s32[2048]{0:T(1024)S(1)} %pad_clamp_fusion), kind=kCustom, calls=%fused_computation | custom fusion | bytes 6297600 | tf_op jit(solution)/shard_map/jit(_take)/gather | solution.py:68
  56.7 0.0 copy-done
  56.7 3.2 fusion.18
  59.9 25.9 %pmax.14 = f32[1536]{0:T(1024)S(1)} all-reduce(f32[1536]{0:T(1024)S(1)} %get-tuple-element.45), channel_id=1, replica_groups=mesh['items'=32,'cents'=16] {'cents'}, use_global_device_ids=true, to_apply=%region_4.5 | all-reduce | flops 1536 | bytes 12288 | tf_op jit(solution)/shard_map/pmax | solution.py:82
  85.8 0.1 fusion.4
  85.9 24.4 %psum.42 = f32[1536]{0:T(1024)S(1)} all-reduce(f32[1536]{0:T(1024)S(1)} %fusion.4), channel_id=1, replica_groups=mesh['items'=32,'cents'=16] {'cents'}, use_global_device_ids=true, to_apply=%region_6.7 | all-reduce | flops 1536 | bytes 12288 | tf_op jit(solution)/shard_map/psum | solution.py:84
  110.3 0.2 convert_reduce_fusion.1
  110.6 3.4 fusion.16
  114.0 0.0 all-reduce.4.cloned.1.call-update
  114.0 0.0 all-reduce.6.cloned.1.call-start
  114.1 107.7 %psum.44 = f32[128]{0:T(128)S(1)} all-reduce(f32[128]{0:T(128)S(1)} %get-tuple-element.41), channel_id=1, replica_groups=mesh['items'=32,'cents'=16] {'items'}, use_global_device_ids=true, to_apply=%region_9.10 | all-reduce | flops 128 | bytes 1024 | tf_op jit(solution)/shard_map/psum | solution.py:90
  221.8 84.7 %all-reduce.4.cloned.1.call-done = f32[128,1024]{1,0:T(8,128)} async-done(((f32[128,1024]{1,0:T(8,128)}), f32[128,1024]{1,0:T(8,128)}) %all-reduce.4.cloned.1.call-update) | async-done | bytes 524304 | tf_op jit(solution)/shard_map/psum | solution.py:90
  306.5 1.3 fusion.10
  307.7 3.2 fusion.19
  310.9 21.5 %pmax.15 = f32[1536]{0:T(1024)S(1)} all-reduce(f32[1536]{0:T(1024)S(1)} %get-tuple-element.47), channel_id=1, replica_groups=mesh['items'=32,'cents'=16] {'cents'}, use_global_device_ids=true, to_apply=%region_12.13 | all-reduce | flops 1536 | bytes 12288 | tf_op jit(solution)/shard_map/pmax | solution.py:82
  332.4 0.1 fusion.5
  332.6 24.4 %psum.45 = f32[1536]{0:T(1024)S(1)} all-reduce(f32[1536]{0:T(1024)S(1)} %fusion.5), channel_id=1, replica_groups=mesh['items'=32,'cents'=16] {'cents'}, use_global_device_ids=true, to_apply=%region_14.15 | all-reduce | flops 1536 | bytes 12288 | tf_op jit(solution)/shard_map/psum | solution.py:84
  357.0 0.2 convert_reduce_fusion
  357.2 3.4 fusion.15
  360.6 0.0 all-reduce.6.cloned.1.call-update
  360.6 72.6 %psum.47 = f32[128]{0:T(128)S(1)} all-reduce(f32[128]{0:T(128)S(1)} %get-tuple-element.37), channel_id=1, replica_groups=mesh['items'=32,'cents'=16] {'items'}, use_global_device_ids=true, to_apply=%region_17.18 | all-reduce | flops 128 | bytes 1024 | tf_op jit(solution)/shard_map/psum | solution.py:90
  433.3 85.3 %all-reduce.6.cloned.1.call-done = f32[128,1024]{1,0:T(8,128)} async-done(((f32[128,1024]{1,0:T(8,128)}), f32[128,1024]{1,0:T(8,128)}) %all-reduce.6.cloned.1.call-update) | async-done | bytes 524304 | tf_op jit(solution)/shard_map/psum | solution.py:90
  518.6 1.9 fusion.13
  (7 shorter events, 0.1 us)
Async XLA Ops:
  6.5 300.0 %all-reduce.4.cloned.1.call-start = ((), (), s32[]{:S(2)}) async-start(), calls=%async_computation | async-start | bytes 1048576 | tf_op jit(solution)/shard_map/psum | solution.py:90
  8.5 33.6 %collective-permute-start = (bf16[192,1024]{1,0:T(8,128)(2,1)S(1)}, bf16[192,1024]{1,0:T(8,128)(2,1)S(1)}, u32[]{:S(2)}, u32[]{:S(2)}) collective-permute-start(bf16[192,1024]{1,0:T(8,128)(2,1)S(1)} %get-tuple-element.43), channel_id=1, source_target_pairs={{0,16},{16,32},{32,48},{48,64},{64,80},{80,96},{96,112},{112,128},... | collective-permute-start | bytes 1179656 | tf_op jit(solution)/shard_map/ppermute | solution.py:29
  12.0 30.1 %collective-permute-start.1 = (bf16[192,1024]{1,0:T(8,128)(2,1)S(1)}, bf16[192,1024]{1,0:T(8,128)(2,1)S(1)}, u32[]{:S(2)}, u32[]{:S(2)}) collective-permute-start(bf16[192,1024]{1,0:T(8,128)(2,1)S(1)} %get-tuple-element.44), channel_id=1, source_target_pairs={{16,0},{32,16},{48,32},{64,48},{80,64},{96,80},{112,96},{128,112},... | collective-permute-start | bytes 1179656 | tf_op jit(solution)/shard_map/ppermute | solution.py:32
  46.0 10.8 %copy-start = (bf16[128,1024]{1,0:T(8,128)(2,1)S(1)}, bf16[128,1024]{1,0:T(8,128)(2,1)}, u32[]{:S(2)}) copy-start(bf16[128,1024]{1,0:T(8,128)(2,1)} %param.7) | copy-start | bytes 786436
  114.0 404.6 %all-reduce.6.cloned.1.call-start = ((), (), s32[]{:S(2)}) async-start(), calls=%async_computation.1 | async-start | bytes 1048576 | tf_op jit(solution)/shard_map/psum | solution.py:90
Sparse Core Ops, SparseCore 0:
  114.2 192.2 all-reduce.3
  360.8 157.7 all-reduce.5
where the time goes:
time: 528 us; the launch traced here: 527 us
  blocking collectives  302 us (57%)
  waiting for transfers between devices  170 us (32%)
  between operations  14.2 us (3%)
  local copies, waits for them, and re-layouts  14.1 us (3%)
  matrix products  13.2 us (2%)
  other arithmetic  8.94 us (2%)
    psum x2, blocking collectives, body(): moment, mass = lax.psum((moment_here, mass_here), 'items')  180 us
    psum x2, waiting for transfers between devices, body(): moment, mass = lax.psum((moment_here, mass_here), 'items')  170 us
    psum x2, blocking collectives, body(): total = lax.psum(jnp.sum(expo, axis=1), 'cents')  48.8 us
    pmax x2, blocking collectives, body(): top = lax.pmax(jnp.max(score, axis=1), 'cents')  47.4 us
    unnamed x1, blocking collectives  25.5 us
    gather x1, local copies, waits for them, and re-layouts, settle_rows(): return jnp.take(joined, source, axis=0)  10.8 us
  transfers between devices with their start and end apart: 4, of which 2 were waited for; matrix products, arithmetic and copies ran while one was open for 1% of the time, Pallas kernels for 0%

commit v1 on v0

--- a/solution.py
+++ b/solution.py
@@ -81,7 +81,9 @@
         score = (2.0 * dots - norms[None, :]) * scale
         top = lax.pmax(jnp.max(score, axis=1), "cents")
         expo = jnp.exp(score - top[:, None])
-        total = lax.psum(jnp.sum(expo, axis=1), "cents")
+        own = jnp.sum(expo, axis=1)
+        shards = lax.all_gather(own, "cents", axis=0, tiled=False)
+        total = shards.sum(axis=0)
         resp = (expo / total[:, None]).astype(jnp.bfloat16)
         mass_here = jnp.sum(resp.astype(jnp.float32), axis=0)
         moment_here = lax.dot_general(

time: 528 us -> 510 us (0.966)
  blocking collectives: 302 us -> 290 us
  waiting for transfers between devices: 170 us -> 164 us
    psum x2 -> x0, blocking collectives: 48.8 us -> none  [body(): total = lax.psum(jnp.sum(expo, axis=1), 'cents')]
    all_gather x0 -> x2, blocking collectives: none -> 36.5 us  [body(): shards = lax.all_gather(own, 'cents', axis=0, tiled=False)]
    psum x2, waiting for transfers between devices: 170 us -> 164 us  [body(): moment, mass = lax.psum((moment_here, mass_here), 'items')]
where the time goes in v1:
time: 510 us; the launch traced here: 509 us
  blocking collectives  290 us (57%)
  waiting for transfers between devices  164 us (32%)
  between operations  14.2 us (3%)
  local copies, waits for them, and re-layouts  14.1 us (3%)
  matrix products  13.2 us (3%)
  other arithmetic  9.08 us (2%)
    psum x2, blocking collectives, body(): moment, mass = lax.psum((moment_here, mass_here), 'items')  180 us
    psum x2, waiting for transfers between devices, body(): moment, mass = lax.psum((moment_here, mass_here), 'items')  164 us
    pmax x2, blocking collectives, body(): top = lax.pmax(jnp.max(score, axis=1), 'cents')  47.4 us
    all_gather x2, blocking collectives, body(): shards = lax.all_gather(own, 'cents', axis=0, tiled=False)  36.5 us
    unnamed x1, blocking collectives  25.5 us
    gather x1, local copies, waits for them, and re-layouts, settle_rows(): return jnp.take(joined, source, axis=0)  10.8 us
  transfers between devices with their start and end apart: 4, of which 2 were waited for; matrix products, arithmetic and copies ran while one was open for 1% of the time, Pallas kernels for 0%

profile of v1, /device:TPU:64, one launch (start us, length us, event | category | flops | bytes accessed | tf_op | source)
XLA Modules:
  0.0 509.1 jit_solution(4997157799903163296)
XLA Ops:
  6.5 0.0 all-reduce.4.cloned.1.call-start
  7.2 1.3 constant_dynamic-slice_fusion.1
  8.5 3.5 collective-permute-start
  12.0 1.3 collective-permute-start.1
  13.3 1.3 dynamic-slice
  14.6 0.7 dynamic-update-slice
  15.4 25.5 %all-reduce = s32[32]{0:T(128)S(1)} all-reduce(s32[32]{0:T(128)S(1)} %dynamic-update-slice), channel_id=2, replica_groups=mesh['items'=32,'cents'=16] {'items'}, use_global_device_ids=true, to_apply=%add | all-reduce | flops 32 | bytes 256
  40.9 1.1 fusion.6
  42.0 0.0 collective-permute-done
  42.0 0.0 collective-permute-done.1
  42.0 3.9 pad_maximum_fusion
  46.0 0.0 copy-start
  46.0 10.8 %gather_fusion = bf16[1536,1024]{1,0:T(8,128)(2,1)} fusion(bf16[2304,1024]{1,0:T(8,128)(2,1)} %pad_maximum_fusion, s32[2048]{0:T(1024)S(1)} %pad_clamp_fusion), kind=kCustom, calls=%fused_computation | custom fusion | bytes 6297600 | tf_op jit(solution)/shard_map/jit(_take)/gather | solution.py:68
  56.7 0.0 copy-done
  56.7 3.2 fusion.18
  59.9 25.9 %pmax.14 = f32[1536]{0:T(1024)S(1)} all-reduce(f32[1536]{0:T(1024)S(1)} %get-tuple-element.45), channel_id=1, replica_groups=mesh['items'=32,'cents'=16] {'cents'}, use_global_device_ids=true, to_apply=%region_4.5 | all-reduce | flops 1536 | bytes 12288 | tf_op jit(solution)/shard_map/pmax | solution.py:82
  85.8 0.1 fusion.4
  85.9 17.9 %all-gather.3 = f32[16,1,1536]{2,1,0:T(1,128)S(1)} all-gather(f32[1,1,1536]{2,1,0:T(1,128)S(1)} %reshape.84), channel_id=3, replica_groups=mesh['items'=32,'cents'=16] {'cents'}, dimensions={0}, use_global_device_ids=true | all-gather | bytes 104448 | tf_op jit(solution)/shard_map/all_gather | solution.py:85
  103.8 0.1 reduce_sum.74
  103.9 0.2 convert_reduce_fusion.1
  104.1 3.4 fusion.16
  107.6 0.0 all-reduce.4.cloned.1.call-update
  107.6 0.0 all-reduce.6.cloned.1.call-start
  107.6 107.8 %psum.29 = f32[128]{0:T(128)S(1)} all-reduce(f32[128]{0:T(128)S(1)} %get-tuple-element.41), channel_id=1, replica_groups=mesh['items'=32,'cents'=16] {'items'}, use_global_device_ids=true, to_apply=%region_9.10 | all-reduce | flops 128 | bytes 1024 | tf_op jit(solution)/shard_map/psum | solution.py:92
  215.5 81.8 %all-reduce.4.cloned.1.call-done = f32[128,1024]{1,0:T(8,128)} async-done(((f32[128,1024]{1,0:T(8,128)}), f32[128,1024]{1,0:T(8,128)}) %all-reduce.4.cloned.1.call-update) | async-done | bytes 524304 | tf_op jit(solution)/shard_map/psum | solution.py:92
  297.3 1.3 fusion.10
  298.5 3.2 fusion.19
  301.7 21.5 %pmax.15 = f32[1536]{0:T(1024)S(1)} all-reduce(f32[1536]{0:T(1024)S(1)} %get-tuple-element.47), channel_id=1, replica_groups=mesh['items'=32,'cents'=16] {'cents'}, use_global_device_ids=true, to_apply=%region_12.13 | all-reduce | flops 1536 | bytes 12288 | tf_op jit(solution)/shard_map/pmax | solution.py:82
  323.2 0.1 fusion.5
  323.4 18.6 %all-gather.4 = f32[16,1,1536]{2,1,0:T(1,128)S(1)} all-gather(f32[1,1,1536]{2,1,0:T(1,128)S(1)} %reshape.86), channel_id=4, replica_groups=mesh['items'=32,'cents'=16] {'cents'}, dimensions={0}, use_global_device_ids=true | all-gather | bytes 104448 | tf_op jit(solution)/shard_map/all_gather | solution.py:85
  342.0 0.1 reduce_sum.78
  342.1 0.2 convert_reduce_fusion
  342.3 3.4 fusion.15
  345.7 0.0 all-reduce.6.cloned.1.call-update
  345.8 72.5 %psum.31 = f32[128]{0:T(128)S(1)} all-reduce(f32[128]{0:T(128)S(1)} %get-tuple-element.37), channel_id=1, replica_groups=mesh['items'=32,'cents'=16] {'items'}, use_global_device_ids=true, to_apply=%region_17.18 | all-reduce | flops 128 | bytes 1024 | tf_op jit(solution)/shard_map/psum | solution.py:92
  418.2 82.2 %all-reduce.6.cloned.1.call-done = f32[128,1024]{1,0:T(8,128)} async-done(((f32[128,1024]{1,0:T(8,128)}), f32[128,1024]{1,0:T(8,128)}) %all-reduce.6.cloned.1.call-update) | async-done | bytes 524304 | tf_op jit(solution)/shard_map/psum | solution.py:92
  500.5 1.9 fusion.13
  (9 shorter events, 0.1 us)
Async XLA Ops:
  6.5 290.8 %all-reduce.4.cloned.1.call-start = ((), (), s32[]{:S(2)}) async-start(), calls=%async_computation | async-start | bytes 1048576 | tf_op jit(solution)/shard_map/psum | solution.py:92
  8.5 33.6 %collective-permute-start = (bf16[192,1024]{1,0:T(8,128)(2,1)S(1)}, bf16[192,1024]{1,0:T(8,128)(2,1)S(1)}, u32[]{:S(2)}, u32[]{:S(2)}) collective-permute-start(bf16[192,1024]{1,0:T(8,128)(2,1)S(1)} %get-tuple-element.43), channel_id=1, source_target_pairs={{0,16},{16,32},{32,48},{48,64},{64,80},{80,96},{96,112},{112,128},... | collective-permute-start | bytes 1179656 | tf_op jit(solution)/shard_map/ppermute | solution.py:29
  12.0 30.1 %collective-permute-start.1 = (bf16[192,1024]{1,0:T(8,128)(2,1)S(1)}, bf16[192,1024]{1,0:T(8,128)(2,1)S(1)}, u32[]{:S(2)}, u32[]{:S(2)}) collective-permute-start(bf16[192,1024]{1,0:T(8,128)(2,1)S(1)} %get-tuple-element.44), channel_id=1, source_target_pairs={{16,0},{32,16},{48,32},{64,48},{80,64},{96,80},{112,96},{128,112},... | collective-permute-start | bytes 1179656 | tf_op jit(solution)/shard_map/ppermute | solution.py:32
  46.0 10.8 %copy-start = (bf16[128,1024]{1,0:T(8,128)(2,1)S(1)}, bf16[128,1024]{1,0:T(8,128)(2,1)}, u32[]{:S(2)}) copy-start(bf16[128,1024]{1,0:T(8,128)(2,1)} %param.7) | copy-start | bytes 786436
  107.6 392.9 %all-reduce.6.cloned.1.call-start = ((), (), s32[]{:S(2)}) async-start(), calls=%async_computation.1 | async-start | bytes 1048576 | tf_op jit(solution)/shard_map/psum | solution.py:92
Sparse Core Ops, SparseCore 0:
  107.7 189.5 all-reduce.3
  345.9 154.5 all-reduce.5
